TPU v7x, 32 devices: a whole 2x2x4 slice. The times are simulated.
32 devices in a mesh: edge: 8 (over y, x, core), feat: 4 (over z).
Axes of the slice: x: 2, y: 2, z: 4, core: 2. Of those that a mesh axis runs over, the one named last changes fastest.
Arguments:
- node_latents: bfloat16 [4, 4096, 256], P('feat', 'edge'), may hold values from -6 to 6
- edge_latents: bfloat16 [4, 32768, 256], P('feat', 'edge'), may hold values from -6 to 6
- senders: int32 [32768], P('edge'), may hold values from 0 to 4095, as said below
- receivers: int32 [32768], P('edge'), may hold values from 0 to 4095, as said below
- regions: int32 [32768], P('edge'), may hold values from 0 to 23
- forced: int32 [4096], P('edge'), may hold values 0 or 1
- params: float32 [1824, 256], P('feat'), may hold values from -1.5 to 1.5, as said below
- first_moment: float32 [1824, 256], P('feat'), may hold values from -0.34 to 0.34
- second_moment: float32 [1824, 256], P('feat'), may hold values from 0.004 to 0.22
- averaged: float32 [1824, 256], P('feat'), may hold values from -1.7 to 1.7
- step: int32 [1], replicated, may hold values from 1 to 20
- cotangent: float32 [4, 4096, 256], P('feat', 'edge'), may hold values from -6 to 6
Outputs:
- new_latents: float32 [4, 4096, 256], P('feat', 'edge')
- grad_latents: float32 [4, 4096, 256], P('feat', 'edge')
- grad_edges: bfloat16 [4, 32768, 256], P('feat', 'edge')
- new_first: float32 [1824, 256], P('feat')
- new_second: float32 [1824, 256], P('feat')
- new_params: float32 [1824, 256], P('feat')
- new_average: float32 [1824, 256], P('feat')
- grad_norm: float32 [1], replicated
- vector_grads: float32 [8, 256], replicated
Inputs may be any that keep to these rules, and one draw needn't show every extreme that they name: `senders`: nodes are numbered so that node block b is nodes b * 512 to (b + 1) * 512 - 1. Edge k lies in edge block e = k // 4096; its sender lies in node block e - 1, e or e + 1, taken cyclically over the 4096 nodes. `receivers`: the receiver of edge k lies in node block e - 1, e or e + 1 of its edge block e = k // 4096, taken cyclically. `params`: parameters scaled by fan-in; gains near one.
All inputs are finite; a program needn't handle non-finite values. No bound on the sum of `forced` on one device may be relied on, other than what follows from the above.
Results may differ from a plain program's by a relative error of at most 0.0039.
The roundings to bfloat16 on the way count: a program that leaves them out, or rounds other values in their place, can miss the bound.
Values may be sent and summed in bfloat16 or wider, within the bound.
No kernel may reach another device: no remote copies, remote signals or barrier semaphores. Data moves between devices by JAX's collectives and lax.ppermute only.
A program may use at most 128 MiB of HBM per device.

v0:
```python
import jax
import jax.numpy as jnp
from jax import lax
from jax.sharding import PartitionSpec as P

NORM_EPS = 1e-05
MAX_NORM = 512.0
RATE = 0.05
BETA_ONE = 0.9
BETA_TWO = 0.95
ADAM_EPS = 1e-08
WEIGHT_DECAY = 0.1
AVERAGE_DECAY = 0.999


def padded(cells, sides, width):
    for axis, dim in sides:
        count = lax.axis_size(axis)
        head = lax.slice_in_dim(cells, 0, width, axis=dim)
        tail = lax.slice_in_dim(cells, cells.shape[dim] - width, cells.shape[dim], axis=dim)
        cells = jnp.concatenate(
            [
                lax.ppermute(tail, axis, [(i, (i + 1) % count) for i in range(count)]),
                cells,
                lax.ppermute(head, axis, [((i + 1) % count, i) for i in range(count)]),
            ],
            axis=dim,
        )
    return cells


def passed_along(value, axis, steps):
    count = lax.axis_size(axis)
    pairs = [(source, (source + steps) % count) for source in range(count)]
    return lax.ppermute(value, axis, pairs)


def product(left, right):
    return jnp.dot(left, right, preferred_element_type=jnp.float32)


def outer_product(left, right):
    return lax.dot_general(
        left, right, (((0,), (0,)), ((), ())), preferred_element_type=jnp.float32
    )


def product_transposed(left, right):
    return lax.dot_general(
        left, right, (((1,), (1,)), ((), ())), preferred_element_type=jnp.float32
    )


def pick_rows(table, indices):
    return jnp.take(table, indices, axis=0)


def add_rows(values, indices, rows):
    return jax.ops.segment_sum(values, indices, num_segments=rows)


def normalized(values):
    center = values - jnp.mean(values, axis=-1, keepdims=True)
    spread = jnp.mean(center * center, axis=-1, keepdims=True)
    inverse = lax.rsqrt(spread + NORM_EPS)
    return (center * inverse, inverse)


def layer_norm(values, gain, shift):
    unit, inverse = normalized(values)
    return unit * gain + shift


def norm_backward(values, gain, upstream):
    unit, inverse = normalized(values)
    scaled = upstream * gain
    inner = (
        scaled
        - jnp.mean(scaled, axis=-1, keepdims=True)
        - unit * jnp.mean(scaled * unit, axis=-1, keepdims=True)
    )
    return (inverse * inner, jnp.sum(upstream * unit, axis=0), jnp.sum(upstream, axis=0))


def silu_slope(values):
    sigma = jax.nn.sigmoid(values)
    return sigma * (1.0 + values * (1.0 - sigma))


def neighbourhood(latents):
    return padded(latents, (("edge", 0),), latents.shape[0])


def on_device(
    node_latents,
    edge_latents,
    senders,
    receivers,
    regions,
    forced,
    params,
    first_moment,
    second_moment,
    averaged,
    step,
    cotangent,
):
    latents = node_latents[0]
    edges = edge_latents[0]
    upstream = cotangent[0]
    width = latents.shape[1]
    node_rows = latents.shape[0]
    total_nodes = node_rows * lax.axis_size("edge")
    lowest = (lax.axis_index("edge") - 1) * node_rows
    send_local = jnp.mod(senders - lowest, total_nodes)
    recv_local = jnp.mod(receivers - lowest, total_nodes)
    weights = lax.all_gather(params.astype(jnp.bfloat16), "feat", axis=0, tiled=True)
    first = weights[0 : 3 * width]
    second = weights[3 * width : 4 * width]
    node_first = weights[4 * width : 6 * width]
    node_second = weights[6 * width : 7 * width]
    vectors = weights[7 * width : 7 * width + 8].astype(jnp.float32)
    table = weights[7 * width + 8 :]
    region_onehot = jax.nn.one_hot(regions, table.shape[0], dtype=jnp.bfloat16)
    near_nodes = neighbourhood(latents)
    from_send = pick_rows(near_nodes, send_local)
    from_recv = pick_rows(near_nodes, recv_local)
    pre = product(from_send, first[0:width]) + product(from_recv, first[width : 2 * width])
    pre = (
        pre
        + product(edges, first[2 * width : 3 * width])
        + vectors[0]
        + product(region_onehot, table)
    )
    hidden = jax.nn.silu(pre).astype(jnp.bfloat16)
    inner = product(hidden, second) + vectors[1]
    from_send, from_recv, pre, hidden, inner = (from_send, from_recv, pre, hidden, inner)
    messages = layer_norm(inner, vectors[2], vectors[3])
    partial_value = add_rows(messages, recv_local, 3 * node_rows)
    from_below = passed_along(partial_value[2 * node_rows :], "edge", 1)
    from_above = passed_along(partial_value[0:node_rows], "edge", -1)
    aggregate = (partial_value[node_rows : 2 * node_rows] + from_below + from_above).astype(
        jnp.bfloat16
    )
    pre_node = (
        product(latents, node_first[0:width])
        + product(aggregate, node_first[width : 2 * width])
        + vectors[4]
    )
    hidden_node = jax.nn.silu(pre_node).astype(jnp.bfloat16)
    inner_node = product(hidden_node, node_second) + vectors[5]
    update = layer_norm(inner_node, vectors[6], vectors[7])
    keep = (1 - forced).astype(jnp.float32)[:, None]
    new_latents = latents.astype(jnp.float32) + keep * update
    d_update = upstream * keep
    d_inner_node, d_gain_node, d_shift_node = norm_backward(inner_node, vectors[6], d_update)
    d_inner_node = d_inner_node.astype(jnp.bfloat16)
    g_node_second = outer_product(hidden_node, d_inner_node)
    d_bias_node_second = jnp.sum(d_inner_node.astype(jnp.float32), axis=0)
    d_pre_node = (product_transposed(d_inner_node, node_second) * silu_slope(pre_node)).astype(
        jnp.bfloat16
    )
    g_node_first = jnp.concatenate(
        [outer_product(latents, d_pre_node), outer_product(aggregate, d_pre_node)], axis=0
    )
    d_bias_node_first = jnp.sum(d_pre_node.astype(jnp.float32), axis=0)
    d_from_nodes = product_transposed(d_pre_node, node_first[0:width])
    d_aggregate = product_transposed(d_pre_node, node_first[width : 2 * width]).astype(jnp.bfloat16)
    near_back = padded(d_aggregate, (("edge", 0),), node_rows)
    d_messages = pick_rows(near_back, recv_local).astype(jnp.float32)
    d_inner, d_gain_edge, d_shift_edge = norm_backward(inner, vectors[2], d_messages)
    d_inner = d_inner.astype(jnp.bfloat16)
    g_second = outer_product(hidden, d_inner)
    d_bias_second = jnp.sum(d_inner.astype(jnp.float32), axis=0)
    d_pre = (product_transposed(d_inner, second) * silu_slope(pre)).astype(jnp.bfloat16)
    g_first = jnp.concatenate(
        [
            outer_product(from_send, d_pre),
            outer_product(from_recv, d_pre),
            outer_product(edges, d_pre),
        ],
        axis=0,
    )
    d_bias_first = jnp.sum(d_pre.astype(jnp.float32), axis=0)
    g_table = outer_product(region_onehot, d_pre)
    d_send = product_transposed(d_pre, first[0:width])
    d_recv = product_transposed(d_pre, first[width : 2 * width])
    grad_edges = product_transposed(d_pre, first[2 * width : 3 * width]).astype(jnp.bfloat16)
    node_partial = add_rows(d_send, send_local, 3 * node_rows) + add_rows(
        d_recv, recv_local, 3 * node_rows
    )
    grads_below = passed_along(
        node_partial[2 * node_rows :].astype(jnp.bfloat16), "edge", 1
    ).astype(jnp.float32)
    grads_above = passed_along(node_partial[0:node_rows].astype(jnp.bfloat16), "edge", -1).astype(
        jnp.float32
    )
    d_nodes = node_partial[node_rows : 2 * node_rows] + grads_below + grads_above
    grad_latents = upstream + d_from_nodes + d_nodes
    vector_rows = jnp.stack(
        [
            d_bias_first,
            d_bias_second,
            d_gain_edge,
            d_shift_edge,
            d_bias_node_first,
            d_bias_node_second,
            d_gain_node,
            d_shift_node,
        ],
        axis=0,
    )
    local_grad = jnp.concatenate(
        [g_first, g_second, g_node_first, g_node_second, vector_rows, g_table], axis=0
    )
    share = params.shape[0]
    summed = lax.psum(local_grad, ("edge", "feat"))
    owned = lax.dynamic_slice_in_dim(summed, lax.axis_index("feat") * share, share, 0)
    rows_here = lax.axis_index("feat") * share + lax.broadcasted_iota(jnp.int32, (8, share), 1)
    wanted = 7 * width + lax.broadcasted_iota(jnp.int32, (8, share), 0)
    select = (rows_here == wanted).astype(jnp.float32)
    vector_piece = jnp.dot(
        select, owned, precision=lax.Precision.HIGHEST, preferred_element_type=jnp.float32
    )
    squares, vector_total = lax.psum((jnp.sum(owned * owned), vector_piece), "feat")
    grad_norm = jnp.sqrt(squares)
    factor = jnp.minimum(1.0, MAX_NORM / (grad_norm + 1e-06))
    clipped = owned * factor
    vector_grads = vector_total * factor
    new_first = BETA_ONE * first_moment + (1.0 - BETA_ONE) * clipped
    new_second = BETA_TWO * second_moment + (1.0 - BETA_TWO) * clipped * clipped
    count_steps = step[0].astype(jnp.float32)
    first_hat = new_first / (1.0 - jnp.power(BETA_ONE, count_steps))
    second_hat = new_second / (1.0 - jnp.power(BETA_TWO, count_steps))
    new_params = params - RATE * (
        first_hat / (jnp.sqrt(second_hat) + ADAM_EPS) + WEIGHT_DECAY * params
    )
    decay_now = jnp.minimum(AVERAGE_DECAY, (1.0 + count_steps) / (10.0 + count_steps))
    new_average = decay_now * averaged + (1.0 - decay_now) * new_params
    return (
        new_latents[None],
        grad_latents[None],
        grad_edges[None],
        new_first,
        new_second,
        new_params,
        new_average,
        grad_norm.reshape(1),
        vector_grads,
    )


def solution(mesh):
    placed = (
        P("feat", "edge", None),
        P("feat", "edge", None),
        P("edge"),
        P("edge"),
        P("edge"),
        P("edge"),
        P("feat", None),
        P("feat", None),
        P("feat", None),
        P("feat", None),
        P(),
        P("feat", "edge", None),
    )
    return jax.shard_map(
        on_device,
        mesh=mesh,
        in_specs=placed,
        out_specs=(
            P("feat", "edge", None),
            P("feat", "edge", None),
            P("feat", "edge", None),
            P("feat", None),
            P("feat", None),
            P("feat", None),
            P("feat", None),
            P(),
            P(),
        ),
        check_vma=False,
    )
```

profile of v0, /device:TPU:0, one launch (start us, length us, event | category | flops | bytes accessed | tf_op | source)
XLA Modules:
  0.0 374.1 jit_solution(12631992785596046417)
XLA Ops:
  7.2 1.2 copy.42
  9.0 2.9 collective-permute-start.1
  12.7 1.0 convert_element_type.71
  13.8 22.2 %all_gather.3 = bf16[1824,256]{1,0:T(8,128)(2,1)S(1)} all-gather(bf16[456,256]{1,0:T(8,128)(2,1)S(1)} %convert_element_type.71), channel_id=1, replica_groups=mesh['edge'=8,'feat'=4] {'feat'}, dimensions={0}, use_global_device_ids=true | all-gather | bytes 1167360 | tf_op jit(solution)/shard_map/all_gather | solution.py:117
  36.0 0.9 copy-done.10
  37.0 0.9 pad_maximum_fusion
  37.9 1.4 copy.43
  39.3 17.0 %gather_fusion = bf16[4096,256]{1,0:T(8,128)(2,1)} fusion(bf16[1536,256]{1,0:T(8,128)(2,1)S(1)} %copy.43, s32[4096]{0:T(1024)S(1)} %fusion.66), kind=kCustom, calls=%fused_computation.clone | custom fusion | bytes 4210688 | tf_op jit(solution)/shard_map/jit(_take)/gather | solution.py:55
  56.4 16.9 %gather_fusion.1 = bf16[4096,256]{1,0:T(8,128)(2,1)} fusion(bf16[1536,256]{1,0:T(8,128)(2,1)S(1)} %copy.43, s32[4096]{0:T(1024)S(1)} %fusion.67), kind=kCustom, calls=%fused_computation.1.clone | custom fusion | bytes 4210688 | tf_op jit(solution)/shard_map/jit(_take)/gather | solution.py:55
  73.3 4.0 %fusion.20 = f32[4096,256]{1,0:T(8,128)S(1)} fusion(bf16[4096,256]{1,0:T(8,128)(2,1)} %gather_fusion, pred[4096]{0:T(1024)(128)(4,1)S(1)} %get-tuple-element.86, bf16[1824,256]{1,0:T(8,128)(2,1)} %copy-done.10), kind=kOutput, calls=%fused_computation.49 | convolution fusion | flops 537919488 | bytes 6426624 | tf_op jit(solution)/shard_map/dot_general | solution.py:39
  77.3 1.7 convolution_add_fusion.3
  79.0 1.7 fusion.3
  80.7 4.0 %multiply_convert_fusion = (bf16[4096,256]{1,0:T(8,128)(2,1)S(1)}, f32[4096,256]{1,0:T(8,128)}) fusion(f32[4096,256]{1,0:T(8,128)S(1)} %fusion.3, bf16[1824,256]{1,0:T(8,128)(2,1)} %copy-done.10, s32[4096]{0:T(1024)S(1)} %copy-done.23), kind=kOutput, calls=%fused_computation.30 | convolution fusion | flops 56721408 | bytes 10514432 | tf_op jit(solution)/shard_map/dot_general | solution.py:39
  84.7 1.8 fusion.82
  87.0 1.5 copy-done.1
  88.5 2.7 multiply_add_fusion
  91.2 5.6 %copy.45 = f32[4096,256]{1,0:T(8,128)} copy(f32[4096,256]{0,1:T(8,128)} %multiply_add_fusion) | data formatting | bytes 8388608 | tf_op jit(solution)/shard_map/add | solution.py:71
  96.8 24.1 %scatter_custom_fusion = f32[1536,256]{1,0:T(8,128)} fusion(s32[4096]{0:T(1024)S(1)} %get-tuple-element.58, f32[4096,256]{1,0:T(8,128)} %copy.45, f32[]{:T(128)} %constant.42.clone.1), kind=kCustom, calls=%fused_computation.57 | custom fusion | flops 1048576 | bytes 1573376 | tf_op jit(solution)/shard_map/scatter-add | solution.py:59
  120.9 2.2 fusion.79
  123.2 2.6 collective-permute-start.3
  126.4 1.2 copy.46
  127.7 1.1 fusion.41
  128.8 8.7 %collective-permute-done.2 = f32[512,256]{1,0:T(8,128)S(1)} collective-permute-done((f32[512,256]{1,0:T(8,128)}, f32[512,256]{1,0:T(8,128)S(1)}, u32[]{:S(2)}, u32[]{:S(2)}) %collective-permute-start.2) | collective-permute-done | bytes 524320 | tf_op jit(solution)/shard_map/ppermute | solution.py:35
  137.5 0.8 copy-done.21
  138.3 1.4 fusion.32
  139.8 1.3 multiply_convert_fusion.2
  141.1 1.2 fusion.83
  142.7 1.1 convert_reduce_fusion.3
  143.8 1.0 fusion.86
  144.8 1.2 convert_reduce_fusion.4
  146.1 1.3 convolution_convert_fusion.1
  147.4 2.6 collective-permute-start.5
  150.0 1.0 fusion.85
  151.0 1.0 convolution_bitcast_fusion
  152.0 4.5 %collective-permute-done.4 = bf16[512,256]{1,0:T(8,128)(2,1)S(1)} collective-permute-done((bf16[512,256]{1,0:T(8,128)(2,1)S(1)}, bf16[512,256]{1,0:T(8,128)(2,1)S(1)}, u32[]{:S(2)}, u32[]{:S(2)}) %collective-permute-start.4) | collective-permute-done | bytes 262176 | tf_op jit(solution)/shard_map/ppermute | solution.py:23
  156.6 16.9 %gather_fusion.2 = bf16[4096,256]{1,0:T(8,128)(2,1)} fusion(bf16[1536,256]{1,0:T(8,128)(2,1)S(1)} %pad_maximum_fusion.1, s32[4096]{0:T(1024)S(1)} %fusion.67), kind=kCustom, calls=%fused_computation.2.clone | custom fusion | bytes 4210688 | tf_op jit(solution)/shard_map/jit(_take)/gather | solution.py:55
  173.5 4.1 %copy.48 = bf16[4096,256]{0,1:T(8,128)(2,1)} copy(bf16[4096,256]{1,0:T(8,128)(2,1)} %gather_fusion.2) | data formatting | bytes 4194304 | tf_op jit(solution)/shard_map/jit(_take)/gather | solution.py:55
  177.6 5.3 %fusion.10 = (f32[256]{0:T(256)S(1)}, f32[4096]{0:T(1024)S(1)}, f32[4096]{0:T(1024)S(1)}, f32[256]{0:T(256)S(1)}) fusion(f32[4096,256]{0,1:T(8,128)} %copy-done.1, f32[4096]{0:T(1024)S(1)} %add_rsqrt_fusion, f32[4096]{0:T(1024)S(1)} %broadcast_multiply_fusion.2, bf16[4096,256]{0,1:T(8,128)(2,1)} %copy.48, pred[4096]{0:T(1024)(128)(4,1)S(1)} %get-tuple-element.57, ...), kind=kLoop, calls=%fused_computation.25 | loop fusion | flops 11525632 | bytes 6364160 | tf_op jit(solution)/shard_map/reduce_sum | solution.py:82
  183.0 2.3 convert_reduce_fusion.1
  185.3 1.5 fusion.84
  186.8 0.8 copy-done.25
  187.6 3.0 convert_reduce_fusion.2
  190.6 2.1 fusion.19
  192.9 2.1 fusion.21
  195.1 1.7 fusion.16
  197.1 3.6 fusion.53
  200.8 3.8 %fusion.56 = f32[4096,256]{1,0:T(8,128)} fusion(bf16[4096,256]{1,0:T(8,128)(2,1)S(1)} %get-tuple-element.83, bf16[1824,256]{1,0:T(8,128)(2,1)} %copy-done.10), kind=kOutput, calls=%fused_computation.106 | convolution fusion | flops 536870912 | bytes 6422528 | tf_op jit(solution)/shard_map/dot_general | solution.py:49
  204.6 10.1 %concatenate.11 = f32[1824,256]{1,0:T(8,128)} concatenate(f32[256,256]{1,0:T(8,128)} %fusion.19, f32[256,256]{1,0:T(8,128)} %fusion.21, f32[256,256]{1,0:T(8,128)} %fusion.16, f32[256,256]{1,0:T(8,128)} %fusion.84, f32[256,256]{1,0:T(8,128)S(1)} %copy-done.20, f32[256,256]{1,0:T(8,128)S(1)} %copy-done.19, f32[256,256]{1,0:T(8,128)S(1)} %copy-done.18, f32[1,256]{1,0:T(1,128)S(1)} %bitcast.104, ...), dimensions={0} | concatenate | bytes 3735552 | tf_op jit(solution)/shard_map/concatenate | solution.py:213
  214.7 24.0 %scatter_custom_fusion.2 = f32[1536,256]{1,0:T(8,128)} fusion(s32[4096]{0:T(1024)S(1)} %get-tuple-element.58, f32[4096,256]{1,0:T(8,128)} %fusion.53, f32[]{:T(128)} %constant.42.clone.1), kind=kCustom, calls=%fused_computation.53 | custom fusion | flops 1048576 | bytes 1573376 | tf_op jit(solution)/shard_map/scatter-add | solution.py:59
  238.8 3.1 copy.50
  241.9 24.0 %scatter_custom_fusion.1 = f32[1536,256]{1,0:T(8,128)} fusion(s32[4096]{0:T(1024)S(1)} %get-tuple-element.87, f32[4096,256]{1,0:T(8,128)} %fusion.56, f32[]{:T(128)} %constant.42.clone.1), kind=kCustom, calls=%fused_computation.55 | custom fusion | flops 1048576 | bytes 1573376 | tf_op jit(solution)/shard_map/scatter-add | solution.py:59
  265.9 3.1 copy.49
  269.0 3.4 fusion.78
  272.4 0.8 fusion.80
  273.2 2.6 collective-permute-start.7
  277.1 1.0 copy.51
  278.1 3.7 fusion.5
  282.0 1.4 fusion.30
  283.5 61.5 %all-reduce.3.cloned.1.call-done = f32[1824,256]{1,0:T(8,128)} async-done(((f32[1824,256]{1,0:T(8,128)}), f32[1824,256]{1,0:T(8,128)}) %all-reduce.3.cloned.1.call-update) | async-done | bytes 1867792 | tf_op jit(solution)/shard_map/psum | solution.py:217
  344.9 1.7 multiply_reduce_fusion.4
  346.7 1.9 fusion.38
  348.6 1.0 copy.52
  349.6 12.4 %all-reduce = (f32[]{:T(128)}, f32[8,256]{1,0:T(8,128)S(1)}) all-reduce(f32[]{:T(128)} %multiply_reduce_fusion.4, f32[8,256]{1,0:T(8,128)} %fusion.38), channel_id=1, replica_groups=mesh['edge'=8,'feat'=4] {'feat'}, use_global_device_ids=true, to_apply=%region_21.23 | all-reduce | flops 2049 | bytes 16392 | tf_op jit(solution)/shard_map/psum | solution.py:225
  363.3 2.8 multiply_add_fusion.1
  (82 shorter events, 5.0 us)
Async XLA Ops:
  7.2 71.8 %copy-start = (bf16[1,4096,256]{2,1,0:T(8,128)(2,1)S(1)}, bf16[1,4096,256]{2,1,0:T(8,128)(2,1)}, u32[]{:S(2)}) copy-start(bf16[1,4096,256]{2,1,0:T(8,128)(2,1)} %param.15) | copy-start | bytes 6291460
  7.2 337.8 %all-reduce.3.cloned.1.call-start = ((), (), s32[]{:S(2)}) async-start(), calls=%async_computation | async-start | bytes 3735552 | tf_op jit(solution)/shard_map/psum | solution.py:217
  8.5 28.5 %copy-start.14 = (bf16[1,512,256]{1,2,0:T(8,128)(2,1)}, bf16[1,512,256]{1,2,0:T(8,128)(2,1)S(1)}, u32[]{:S(2)}) copy-start(bf16[1,512,256]{1,2,0:T(8,128)(2,1)S(1)} %copy.42) | copy-start | bytes 786436
  8.5 28.5 %collective-permute-start = (bf16[512,256]{0,1:T(8,128)(2,1)S(1)}, bf16[512,256]{0,1:T(8,128)(2,1)S(1)}, u32[]{:S(2)}, u32[]{:S(2)}) collective-permute-start(bf16[512,256]{0,1:T(8,128)(2,1)S(1)} %bitcast.84), channel_id=1, source_target_pairs={{0,4},{4,8},{8,12},{12,16},{16,20},{20,24},{24,28},{28,0},{1,5},{5... | collective-permute-start | bytes 786440 | tf_op jit(solution)/shard_map/ppermute | solution.py:23
  9.0 28.0 %collective-permute-start.1 = (bf16[512,256]{0,1:T(8,128)(2,1)S(1)}, bf16[512,256]{0,1:T(8,128)(2,1)S(1)}, u32[]{:S(2)}, u32[]{:S(2)}) collective-permute-start(bf16[512,256]{0,1:T(8,128)(2,1)S(1)} %bitcast.85), channel_id=1, source_target_pairs={{4,0},{8,4},{12,8},{16,12},{20,16},{24,20},{28,24},{0,28},{5,1},{9... | collective-permute-start | bytes 786440 | tf_op jit(solution)/shard_map/ppermute | solution.py:25
  36.0 0.9 copy-start.10
  73.3 4.0 %copy-start.8 = (bf16[4096,256]{1,0:T(8,128)(2,1)S(1)}, bf16[4096,256]{1,0:T(8,128)(2,1)}, u32[]{:S(2)}) copy-start(bf16[4096,256]{1,0:T(8,128)(2,1)} %gather_fusion.1) | copy-start | bytes 6291460
  79.0 1.7 copy-start.23
  84.7 1.8 copy-start.6
  86.5 2.0 copy-start.1
  96.8 30.8 %copy-start.24 = (s32[512]{0:T(512)S(1)}, s32[512]{0:T(512)}, u32[]{:S(2)}) copy-start(s32[512]{0:T(512)} %param.19) | copy-start | bytes 6148
  96.8 30.8 %copy-start.13 = (bf16[1,512,256]{2,1,0:T(8,128)(2,1)S(1)}, bf16[1,512,256]{2,1,0:T(8,128)(2,1)}, u32[]{:S(2)}) copy-start(bf16[1,512,256]{2,1,0:T(8,128)(2,1)} %param.14) | copy-start | bytes 786436
  123.2 14.4 %collective-permute-start.2 = (f32[512,256]{1,0:T(8,128)}, f32[512,256]{1,0:T(8,128)S(1)}, u32[]{:S(2)}, u32[]{:S(2)}) collective-permute-start(f32[512,256]{1,0:T(8,128)} %get-tuple-element.61), channel_id=1, source_target_pairs={{0,4},{4,8},{8,12},{12,16},{16,20},{20,24},{24,28},{28,0},{1,5},{5... | collective-permute-start | bytes 1572872 | tf_op jit(solution)/shard_map/ppermute | solution.py:35
  123.2 15.2 %collective-permute-start.3 = (f32[512,256]{1,0:T(8,128)}, f32[512,256]{1,0:T(8,128)}, u32[]{:S(2)}, u32[]{:S(2)}) collective-permute-start(f32[512,256]{1,0:T(8,128)} %get-tuple-element.62), channel_id=1, source_target_pairs={{0,28},{4,0},{8,4},{12,8},{16,12},{20,16},{24,20},{28,24},{1,29},{... | collective-permute-start | bytes 1572872 | tf_op jit(solution)/shard_map/ppermute | solution.py:35
  137.5 0.8 copy-start.21
  139.8 2.9 copy-start.15
  146.0 10.5 %copy-start.11 = (bf16[512,256]{1,0:T(8,128)(2,1)}, bf16[512,256]{1,0:T(8,128)(2,1)S(1)}, u32[]{:S(2)}) copy-start(bf16[512,256]{1,0:T(8,128)(2,1)S(1)} %get-tuple-element.85) | copy-start | bytes 786436
  147.3 9.2 %collective-permute-start.4 = (bf16[512,256]{1,0:T(8,128)(2,1)S(1)}, bf16[512,256]{1,0:T(8,128)(2,1)S(1)}, u32[]{:S(2)}, u32[]{:S(2)}) collective-permute-start(bf16[512,256]{1,0:T(8,128)(2,1)S(1)} %convolution_convert_fusion.1), channel_id=1, source_target_pairs={{0,4},{4,8},{8,12},{12,16},{16,20},{20,24},{24,28},{28,0},{1,5},{5... | collective-permute-start | bytes 786440 | tf_op jit(solution)/shard_map/ppermute | solution.py:23
  147.4 9.1 %collective-permute-start.5 = (bf16[512,256]{1,0:T(8,128)(2,1)S(1)}, bf16[512,256]{1,0:T(8,128)(2,1)S(1)}, u32[]{:S(2)}, u32[]{:S(2)}) collective-permute-start(bf16[512,256]{1,0:T(8,128)(2,1)S(1)} %convolution_convert_fusion.1), channel_id=1, source_target_pairs={{4,0},{8,4},{12,8},{16,12},{20,16},{24,20},{28,24},{0,28},{5,1},{9... | collective-permute-start | bytes 786440 | tf_op jit(solution)/shard_map/ppermute | solution.py:25
  177.6 5.4 %copy-start.2 = (f32[4096,256]{0,1:T(8,128)S(1)}, f32[4096,256]{0,1:T(8,128)}, u32[]{:S(2)}) copy-start(f32[4096,256]{0,1:T(8,128)} %copy-done.1) | copy-start | bytes 12582916
  177.6 5.4 %copy-start.4 = (bf16[4096,256]{0,1:T(8,128)(2,1)S(1)}, bf16[4096,256]{0,1:T(8,128)(2,1)}, u32[]{:S(2)}) copy-start(bf16[4096,256]{0,1:T(8,128)(2,1)} %copy.48) | copy-start | bytes 6291460
  183.0 2.3 copy-start.7
  185.3 2.3 copy-start.25
  187.6 3.0 copy-start.5
  190.6 10.2 %copy-start.3 = (bf16[4096,256]{1,0:T(8,128)(2,1)}, bf16[4096,256]{1,0:T(8,128)(2,1)S(1)}, u32[]{:S(2)}) copy-start(bf16[4096,256]{1,0:T(8,128)(2,1)S(1)} %get-tuple-element.83) | copy-start | bytes 6291460
  190.6 2.3 copy-start.9
  200.8 3.8 %copy-start.18 = (f32[256,256]{1,0:T(8,128)S(1)}, f32[256,256]{1,0:T(8,128)}, u32[]{:S(2)}) copy-start(f32[256,256]{1,0:T(8,128)} %fusion.86) | copy-start | bytes 786436
  200.8 3.8 %copy-start.19 = (f32[256,256]{1,0:T(8,128)S(1)}, f32[256,256]{1,0:T(8,128)}, u32[]{:S(2)}) copy-start(f32[256,256]{1,0:T(8,128)} %fusion.85) | copy-start | bytes 786436
  200.8 3.8 %copy-start.20 = (f32[256,256]{1,0:T(8,128)S(1)}, f32[256,256]{1,0:T(8,128)}, u32[]{:S(2)}) copy-start(f32[256,256]{1,0:T(8,128)} %convolution_bitcast_fusion) | copy-start | bytes 786436
  269.0 8.2 %copy-start.16 = (f32[1,512,256]{1,2,0:T(8,128)S(1)}, f32[1,512,256]{1,2,0:T(8,128)}, u32[]{:S(2)}) copy-start(f32[1,512,256]{1,2,0:T(8,128)} %get-tuple-element.65) | copy-start | bytes 1572868
  273.2 8.8 %collective-permute-start.6 = (bf16[512,256]{0,1:T(8,128)(2,1)}, bf16[512,256]{0,1:T(8,128)(2,1)S(1)}, u32[]{:S(2)}, u32[]{:S(2)}) collective-permute-start(bf16[512,256]{0,1:T(8,128)(2,1)} %get-tuple-element.63), channel_id=1, source_target_pairs={{0,4},{4,8},{8,12},{12,16},{16,20},{20,24},{24,28},{28,0},{1,5},{5... | collective-permute-start | bytes 786440 | tf_op jit(solution)/shard_map/ppermute | solution.py:35
  273.2 8.8 %collective-permute-start.7 = (bf16[512,256]{0,1:T(8,128)(2,1)}, bf16[512,256]{0,1:T(8,128)(2,1)}, u32[]{:S(2)}, u32[]{:S(2)}) collective-permute-start(bf16[512,256]{0,1:T(8,128)(2,1)} %get-tuple-element.64), channel_id=1, source_target_pairs={{0,28},{4,0},{8,4},{12,8},{16,12},{20,16},{24,20},{28,24},{1,29},{... | collective-permute-start | bytes 786440 | tf_op jit(solution)/shard_map/ppermute | solution.py:35
  278.1 3.9 %copy-start.12 = (bf16[512,256]{1,0:T(8,128)(2,1)S(1)}, bf16[512,256]{1,0:T(8,128)(2,1)}, u32[]{:S(2)}) copy-start(bf16[512,256]{1,0:T(8,128)(2,1)} %copy-done.11) | copy-start | bytes 786436
  283.5 79.8 %copy-start.17 = (f32[456,256]{1,0:T(8,128)S(1)}, f32[456,256]{1,0:T(8,128)}, u32[]{:S(2)}) copy-start(f32[456,256]{1,0:T(8,128)} %param.20) | copy-start | bytes 1400836
  283.5 79.8 %copy-start.22 = (f32[456,256]{1,0:T(8,128)S(1)}, f32[456,256]{1,0:T(8,128)}, u32[]{:S(2)}) copy-start(f32[456,256]{1,0:T(8,128)} %param.23) | copy-start | bytes 1400836
Sparse Core Ops, SparseCore 0:
  214.8 130.0 all-reduce.2
where the time goes:
time: 375 us; the launch traced here: 374 us
  other arithmetic  98.5 us (26%)
  local copies, waits for them, and re-layouts  90 us (24%)
  waiting for transfers between devices  74.9 us (20%)
  matrix products  47.4 us (13%)
  blocking collectives  34.6 us (9%)
  between operations  17.2 us (5%)
  starting transfers between devices  11.5 us (3%)
    scatter-add x3, other arithmetic, add_rows(): return jax.ops.segment_sum(values, indices, num_segments=rows)  72.2 us
    psum x1, waiting for transfers between devices, on_device(): summed = lax.psum(local_grad, ('edge', 'feat'))  61.5 us
    gather x4, local copies, waits for them, and re-layouts, pick_rows(): return jnp.take(table, indices, axis=0)  55 us
    all_gather x1, blocking collectives, on_device(): lax.all_gather(params.astype(jnp.bfloat16), 'feat', axis=0, tiled=True)  22.2 us
    dot_general x7, matrix products, product_transposed(): lax.dot_general(left, right, (((1,), (1,)), ((), ())), preferred_element_...  18 us
    dot_general x8, matrix products, product(): return jnp.dot(left, right, preferred_element_type=jnp.float32)  16.7 us
    psum x1, blocking collectives, on_device(): lax.psum((jnp.sum(owned * owned), vector_piece), 'feat')  12.4 us
    dot_general x8, matrix products, outer_product(): lax.dot_general(left, right, (((0,), (0,)), ((), ())), preferred_element_...  10.7 us
  transfers between devices with their start and end apart: 9, of which 4 were waited for; matrix products, arithmetic and copies ran while one was open for 19% of the time, Pallas kernels for 0%

commit v1 on v0

--- a/solution.py
+++ b/solution.py
@@ -214,7 +214,7 @@
         [g_first, g_second, g_node_first, g_node_second, vector_rows, g_table], axis=0
     )
     share = params.shape[0]
-    summed = lax.psum(local_grad, ("edge", "feat"))
+    summed = lax.psum(lax.psum(local_grad, "feat"), "edge")
     owned = lax.dynamic_slice_in_dim(summed, lax.axis_index("feat") * share, share, 0)
     rows_here = lax.axis_index("feat") * share + lax.broadcasted_iota(jnp.int32, (8, share), 1)
     wanted = 7 * width + lax.broadcasted_iota(jnp.int32, (8, share), 0)

time: 375 us -> 380 us (1.013)
    ppermute x4, waiting for transfers between devices: 8.93 us -> 13.6 us  [passed_along(): return lax.ppermute(value, axis, pairs)]
    psum x1 -> x2, waiting for transfers between devices: 61.5 us -> 59 us  [on_device(): summed = lax.psum(lax.psum(local_grad, 'feat'), 'edge')]
  transfers between devices with their start and end apart: 9 -> 10, of which waited for: 4 -> 6; matrix products, arithmetic and copies ran while one was open for 19% -> 21% of each run, Pallas kernels for 0% -> 0%
where the time goes in v1:
time: 380 us; the launch traced here: 379 us
  other arithmetic  98.4 us (26%)
  local copies, waits for them, and re-layouts  90.7 us (24%)
  waiting for transfers between devices  77.1 us (20%)
  matrix products  48.5 us (13%)
  blocking collectives  34.9 us (9%)
  between operations  17.2 us (5%)
  starting transfers between devices  11.7 us (3%)
    scatter-add x3, other arithmetic, add_rows(): return jax.ops.segment_sum(values, indices, num_segments=rows)  72.2 us
    psum x2, waiting for transfers between devices, on_device(): summed = lax.psum(lax.psum(local_grad, 'feat'), 'edge')  59 us
    gather x4, local copies, waits for them, and re-layouts, pick_rows(): return jnp.take(table, indices, axis=0)  55 us
    all_gather x1, blocking collectives, on_device(): lax.all_gather(params.astype(jnp.bfloat16), 'feat', axis=0, tiled=True)  22.2 us
    dot_general x7, matrix products, product_transposed(): lax.dot_general(left, right, (((1,), (1,)), ((), ())), preferred_element_...  19.1 us
    dot_general x8, matrix products, product(): return jnp.dot(left, right, preferred_element_type=jnp.float32)  16.7 us
    ppermute x4, waiting for transfers between devices, passed_along(): return lax.ppermute(value, axis, pairs)  13.6 us
    psum x1, blocking collectives, on_device(): lax.psum((jnp.sum(owned * owned), vector_piece), 'feat')  12.6 us
  transfers between devices with their start and end apart: 10, of which 6 were waited for; matrix products, arithmetic and copies ran while one was open for 21% of the time, Pallas kernels for 0%

profile of v1, /device:TPU:0, one launch (start us, length us, event | category | flops | bytes accessed | tf_op | source)
XLA Modules:
  0.0 378.6 jit_solution(9382470679849543556)
XLA Ops:
  7.2 1.2 copy.42
  9.0 2.9 collective-permute-start.1
  12.7 1.0 convert_element_type.71
  13.8 22.2 %all_gather.3 = bf16[1824,256]{1,0:T(8,128)(2,1)S(1)} all-gather(bf16[456,256]{1,0:T(8,128)(2,1)S(1)} %convert_element_type.71), channel_id=1, replica_groups=mesh['edge'=8,'feat'=4] {'feat'}, dimensions={0}, use_global_device_ids=true | all-gather | bytes 1167360 | tf_op jit(solution)/shard_map/all_gather | solution.py:117
  36.0 0.9 copy-done.10
  37.0 0.9 pad_maximum_fusion
  37.9 1.4 copy.43
  39.3 17.0 %gather_fusion = bf16[4096,256]{1,0:T(8,128)(2,1)} fusion(bf16[1536,256]{1,0:T(8,128)(2,1)S(1)} %copy.43, s32[4096]{0:T(1024)S(1)} %fusion.66), kind=kCustom, calls=%fused_computation.clone | custom fusion | bytes 4210688 | tf_op jit(solution)/shard_map/jit(_take)/gather | solution.py:55
  56.4 16.9 %gather_fusion.1 = bf16[4096,256]{1,0:T(8,128)(2,1)} fusion(bf16[1536,256]{1,0:T(8,128)(2,1)S(1)} %copy.43, s32[4096]{0:T(1024)S(1)} %fusion.67), kind=kCustom, calls=%fused_computation.1.clone | custom fusion | bytes 4210688 | tf_op jit(solution)/shard_map/jit(_take)/gather | solution.py:55
  73.3 4.0 %fusion.20 = f32[4096,256]{1,0:T(8,128)S(1)} fusion(bf16[4096,256]{1,0:T(8,128)(2,1)} %gather_fusion, pred[4096]{0:T(1024)(128)(4,1)S(1)} %get-tuple-element.86, bf16[1824,256]{1,0:T(8,128)(2,1)} %copy-done.10), kind=kOutput, calls=%fused_computation.49 | convolution fusion | flops 537919488 | bytes 6426624 | tf_op jit(solution)/shard_map/dot_general | solution.py:39
  77.3 1.7 convolution_add_fusion.3
  79.0 1.7 fusion.3
  80.7 4.0 %multiply_convert_fusion = (bf16[4096,256]{1,0:T(8,128)(2,1)S(1)}, f32[4096,256]{1,0:T(8,128)}) fusion(f32[4096,256]{1,0:T(8,128)S(1)} %fusion.3, bf16[1824,256]{1,0:T(8,128)(2,1)} %copy-done.10, s32[4096]{0:T(1024)S(1)} %copy-done.23), kind=kOutput, calls=%fused_computation.30 | convolution fusion | flops 56721408 | bytes 10514432 | tf_op jit(solution)/shard_map/dot_general | solution.py:39
  84.7 1.8 fusion.82
  87.0 1.5 copy-done.1
  88.5 2.7 multiply_add_fusion
  91.2 5.6 %copy.45 = f32[4096,256]{1,0:T(8,128)} copy(f32[4096,256]{0,1:T(8,128)} %multiply_add_fusion) | data formatting | bytes 8388608 | tf_op jit(solution)/shard_map/add | solution.py:71
  96.8 24.1 %scatter_custom_fusion = f32[1536,256]{1,0:T(8,128)} fusion(s32[4096]{0:T(1024)S(1)} %get-tuple-element.58, f32[4096,256]{1,0:T(8,128)} %copy.45, f32[]{:T(128)} %constant.42.clone.1), kind=kCustom, calls=%fused_computation.57 | custom fusion | flops 1048576 | bytes 1573376 | tf_op jit(solution)/shard_map/scatter-add | solution.py:59
  120.9 2.2 fusion.79
  123.2 2.6 collective-permute-start.3
  125.8 1.2 copy.46
  127.1 1.1 fusion.41
  128.2 9.3 %collective-permute-done.2 = f32[512,256]{1,0:T(8,128)S(1)} collective-permute-done((f32[512,256]{1,0:T(8,128)}, f32[512,256]{1,0:T(8,128)S(1)}, u32[]{:S(2)}, u32[]{:S(2)}) %collective-permute-start.2) | collective-permute-done | bytes 524320 | tf_op jit(solution)/shard_map/ppermute | solution.py:35
  138.4 1.4 fusion.32
  139.8 1.3 multiply_convert_fusion.2
  141.1 1.2 fusion.83
  142.7 1.1 convert_reduce_fusion.3
  143.8 1.0 fusion.86
  144.8 1.2 convert_reduce_fusion.4
  146.1 1.3 convolution_convert_fusion.1
  147.4 2.6 collective-permute-start.5
  150.0 1.0 fusion.85
  151.0 1.0 convolution_bitcast_fusion
  152.0 4.5 %collective-permute-done.4 = bf16[512,256]{1,0:T(8,128)(2,1)S(1)} collective-permute-done((bf16[512,256]{1,0:T(8,128)(2,1)S(1)}, bf16[512,256]{1,0:T(8,128)(2,1)S(1)}, u32[]{:S(2)}, u32[]{:S(2)}) %collective-permute-start.4) | collective-permute-done | bytes 262176 | tf_op jit(solution)/shard_map/ppermute | solution.py:23
  156.6 16.9 %gather_fusion.2 = bf16[4096,256]{1,0:T(8,128)(2,1)} fusion(bf16[1536,256]{1,0:T(8,128)(2,1)S(1)} %pad_maximum_fusion.1, s32[4096]{0:T(1024)S(1)} %fusion.67), kind=kCustom, calls=%fused_computation.2.clone | custom fusion | bytes 4210688 | tf_op jit(solution)/shard_map/jit(_take)/gather | solution.py:55
  173.5 4.1 %copy.48 = bf16[4096,256]{0,1:T(8,128)(2,1)} copy(bf16[4096,256]{1,0:T(8,128)(2,1)} %gather_fusion.2) | data formatting | bytes 4194304 | tf_op jit(solution)/shard_map/jit(_take)/gather | solution.py:55
  177.6 5.3 %fusion.10 = (f32[256]{0:T(256)S(1)}, f32[4096]{0:T(1024)S(1)}, f32[4096]{0:T(1024)S(1)}, f32[256]{0:T(256)S(1)}) fusion(f32[4096,256]{0,1:T(8,128)} %copy-done.1, f32[4096]{0:T(1024)S(1)} %add_rsqrt_fusion, f32[4096]{0:T(1024)S(1)} %broadcast_multiply_fusion.2, bf16[4096,256]{0,1:T(8,128)(2,1)} %copy.48, pred[4096]{0:T(1024)(128)(4,1)S(1)} %get-tuple-element.57, ...), kind=kLoop, calls=%fused_computation.25 | loop fusion | flops 11525632 | bytes 6364160 | tf_op jit(solution)/shard_map/reduce_sum | solution.py:82
  183.0 2.3 convert_reduce_fusion.1
  185.3 1.5 fusion.84
  187.6 3.0 convert_reduce_fusion.2
  190.6 2.1 fusion.19
  192.9 2.1 fusion.21
  195.1 1.7 fusion.16
  197.9 10.1 %concatenate.11 = f32[1824,256]{1,0:T(8,128)} concatenate(f32[256,256]{1,0:T(8,128)} %fusion.19, f32[256,256]{1,0:T(8,128)} %fusion.21, f32[256,256]{1,0:T(8,128)} %fusion.16, f32[256,256]{1,0:T(8,128)} %fusion.84, f32[256,256]{1,0:T(8,128)S(1)} %copy-done.20, f32[256,256]{1,0:T(8,128)S(1)} %copy-done.19, f32[256,256]{1,0:T(8,128)S(1)} %copy-done.18, f32[1,256]{1,0:T(1,128)S(1)} %bitcast.104, ...), dimensions={0} | concatenate | bytes 3735552 | tf_op jit(solution)/shard_map/concatenate | solution.py:213
  208.8 4.3 %fusion.53 = f32[4096,256]{1,0:T(8,128)} fusion(bf16[4096,256]{1,0:T(8,128)(2,1)} %copy-done.3, bf16[1824,256]{1,0:T(8,128)(2,1)} %copy-done.10), kind=kOutput, calls=%fused_computation.103 | convolution fusion | flops 536870912 | bytes 6422528 | tf_op jit(solution)/shard_map/dot_general | solution.py:49
  213.1 24.0 %scatter_custom_fusion.2 = f32[1536,256]{1,0:T(8,128)} fusion(s32[4096]{0:T(1024)S(1)} %get-tuple-element.58, f32[4096,256]{1,0:T(8,128)} %fusion.53, f32[]{:T(128)} %constant.42.clone.1), kind=kCustom, calls=%fused_computation.53 | custom fusion | flops 1048576 | bytes 1573376 | tf_op jit(solution)/shard_map/scatter-add | solution.py:59
  237.1 3.1 copy.50
  240.2 4.3 %fusion.56 = f32[4096,256]{1,0:T(8,128)} fusion(bf16[4096,256]{1,0:T(8,128)(2,1)} %copy-done.3, bf16[1824,256]{1,0:T(8,128)(2,1)} %copy-done.10), kind=kOutput, calls=%fused_computation.106 | convolution fusion | flops 536870912 | bytes 6422528 | tf_op jit(solution)/shard_map/dot_general | solution.py:49
  244.5 24.0 %scatter_custom_fusion.1 = f32[1536,256]{1,0:T(8,128)} fusion(s32[4096]{0:T(1024)S(1)} %get-tuple-element.87, f32[4096,256]{1,0:T(8,128)} %fusion.56, f32[]{:T(128)} %constant.42.clone.1), kind=kCustom, calls=%fused_computation.55 | custom fusion | flops 1048576 | bytes 1573376 | tf_op jit(solution)/shard_map/scatter-add | solution.py:59
  268.5 3.0 copy.49
  271.6 12.9 %all-reduce.4.cloned.1.call-done = f32[1824,256]{1,0:T(8,128)} async-done(((f32[1824,256]{1,0:T(8,128)}), f32[1824,256]{1,0:T(8,128)}) %all-reduce.4.cloned.1.call-update) | async-done | bytes 1867792 | tf_op jit(solution)/shard_map/psum | solution.py:217
  284.5 3.3 fusion.78
  287.9 0.8 fusion.80
  288.7 2.6 collective-permute-start.7
  292.7 1.0 copy.51
  293.7 3.7 fusion.5
  297.9 3.8 %collective-permute-done.7 = bf16[512,256]{0,1:T(8,128)(2,1)} collective-permute-done((bf16[512,256]{0,1:T(8,128)(2,1)}, bf16[512,256]{0,1:T(8,128)(2,1)}, u32[]{:S(2)}, u32[]{:S(2)}) %collective-permute-start.7) | collective-permute-done | bytes 262176 | tf_op jit(solution)/shard_map/ppermute | solution.py:35
  301.7 1.4 fusion.30
  303.1 46.0 %all-reduce.6.cloned.1.call-done = f32[1824,256]{1,0:T(8,128)} async-done(((f32[1824,256]{1,0:T(8,128)}), f32[1824,256]{1,0:T(8,128)}) %all-reduce.6.cloned.1.call-update) | async-done | bytes 1867792 | tf_op jit(solution)/shard_map/psum | solution.py:217
  349.2 1.7 multiply_reduce_fusion.4
  350.9 1.9 fusion.38
  352.8 1.0 copy.52
  353.8 12.6 %all-reduce = (f32[]{:T(128)}, f32[8,256]{1,0:T(8,128)S(1)}) all-reduce(f32[]{:T(128)} %multiply_reduce_fusion.4, f32[8,256]{1,0:T(8,128)} %fusion.38), channel_id=1, replica_groups=mesh['edge'=8,'feat'=4] {'feat'}, use_global_device_ids=true, to_apply=%region_22.24 | all-reduce | flops 2049 | bytes 16392 | tf_op jit(solution)/shard_map/psum | solution.py:225
  367.8 2.8 multiply_add_fusion.1
  (85 shorter events, 7.9 us)
Async XLA Ops:
  7.2 71.8 %copy-start = (bf16[1,4096,256]{2,1,0:T(8,128)(2,1)S(1)}, bf16[1,4096,256]{2,1,0:T(8,128)(2,1)}, u32[]{:S(2)}) copy-start(bf16[1,4096,256]{2,1,0:T(8,128)(2,1)} %param.15) | copy-start | bytes 6291460
  7.2 277.3 %all-reduce.4.cloned.1.call-start = ((), (), s32[]{:S(2)}) async-start(), calls=%async_computation | async-start | bytes 3735552 | tf_op jit(solution)/shard_map/psum | solution.py:217
  8.5 28.5 %copy-start.14 = (bf16[1,512,256]{1,2,0:T(8,128)(2,1)}, bf16[1,512,256]{1,2,0:T(8,128)(2,1)S(1)}, u32[]{:S(2)}) copy-start(bf16[1,512,256]{1,2,0:T(8,128)(2,1)S(1)} %copy.42) | copy-start | bytes 786436
  8.5 28.5 %collective-permute-start = (bf16[512,256]{0,1:T(8,128)(2,1)S(1)}, bf16[512,256]{0,1:T(8,128)(2,1)S(1)}, u32[]{:S(2)}, u32[]{:S(2)}) collective-permute-start(bf16[512,256]{0,1:T(8,128)(2,1)S(1)} %bitcast.84), channel_id=1, source_target_pairs={{0,4},{4,8},{8,12},{12,16},{16,20},{20,24},{24,28},{28,0},{1,5},{5... | collective-permute-start | bytes 786440 | tf_op jit(solution)/shard_map/ppermute | solution.py:23
  9.0 28.0 %collective-permute-start.1 = (bf16[512,256]{0,1:T(8,128)(2,1)S(1)}, bf16[512,256]{0,1:T(8,128)(2,1)S(1)}, u32[]{:S(2)}, u32[]{:S(2)}) collective-permute-start(bf16[512,256]{0,1:T(8,128)(2,1)S(1)} %bitcast.85), channel_id=1, source_target_pairs={{4,0},{8,4},{12,8},{16,12},{20,16},{24,20},{28,24},{0,28},{5,1},{9... | collective-permute-start | bytes 786440 | tf_op jit(solution)/shard_map/ppermute | solution.py:25
  36.0 0.9 copy-start.10
  73.3 4.0 %copy-start.8 = (bf16[4096,256]{1,0:T(8,128)(2,1)S(1)}, bf16[4096,256]{1,0:T(8,128)(2,1)}, u32[]{:S(2)}) copy-start(bf16[4096,256]{1,0:T(8,128)(2,1)} %gather_fusion.1) | copy-start | bytes 6291460
  79.0 1.7 copy-start.23
  84.7 1.8 copy-start.6
  86.5 2.0 copy-start.1
  96.8 30.2 %copy-start.24 = (s32[512]{0:T(512)S(1)}, s32[512]{0:T(512)}, u32[]{:S(2)}) copy-start(s32[512]{0:T(512)} %param.19) | copy-start | bytes 6148
  96.8 30.2 %copy-start.13 = (bf16[1,512,256]{2,1,0:T(8,128)(2,1)S(1)}, bf16[1,512,256]{2,1,0:T(8,128)(2,1)}, u32[]{:S(2)}) copy-start(bf16[1,512,256]{2,1,0:T(8,128)(2,1)} %param.14) | copy-start | bytes 786436
  123.2 14.4 %collective-permute-start.2 = (f32[512,256]{1,0:T(8,128)}, f32[512,256]{1,0:T(8,128)S(1)}, u32[]{:S(2)}, u32[]{:S(2)}) collective-permute-start(f32[512,256]{1,0:T(8,128)} %get-tuple-element.61), channel_id=1, source_target_pairs={{0,4},{4,8},{8,12},{12,16},{16,20},{20,24},{24,28},{28,0},{1,5},{5... | collective-permute-start | bytes 1572872 | tf_op jit(solution)/shard_map/ppermute | solution.py:35
  123.2 15.2 %collective-permute-start.3 = (f32[512,256]{1,0:T(8,128)}, f32[512,256]{1,0:T(8,128)}, u32[]{:S(2)}, u32[]{:S(2)}) collective-permute-start(f32[512,256]{1,0:T(8,128)} %get-tuple-element.62), channel_id=1, source_target_pairs={{0,28},{4,0},{8,4},{12,8},{16,12},{20,16},{24,20},{28,24},{1,29},{... | collective-permute-start | bytes 1572872 | tf_op jit(solution)/shard_map/ppermute | solution.py:35
  137.6 0.8 copy-start.21
  139.8 2.9 copy-start.15
  146.1 10.4 %copy-start.11 = (bf16[512,256]{1,0:T(8,128)(2,1)}, bf16[512,256]{1,0:T(8,128)(2,1)S(1)}, u32[]{:S(2)}) copy-start(bf16[512,256]{1,0:T(8,128)(2,1)S(1)} %get-tuple-element.85) | copy-start | bytes 786436
  147.3 9.2 %collective-permute-start.4 = (bf16[512,256]{1,0:T(8,128)(2,1)S(1)}, bf16[512,256]{1,0:T(8,128)(2,1)S(1)}, u32[]{:S(2)}, u32[]{:S(2)}) collective-permute-start(bf16[512,256]{1,0:T(8,128)(2,1)S(1)} %convolution_convert_fusion.1), channel_id=1, source_target_pairs={{0,4},{4,8},{8,12},{12,16},{16,20},{20,24},{24,28},{28,0},{1,5},{5... | collective-permute-start | bytes 786440 | tf_op jit(solution)/shard_map/ppermute | solution.py:23
  147.4 9.1 %collective-permute-start.5 = (bf16[512,256]{1,0:T(8,128)(2,1)S(1)}, bf16[512,256]{1,0:T(8,128)(2,1)S(1)}, u32[]{:S(2)}, u32[]{:S(2)}) collective-permute-start(bf16[512,256]{1,0:T(8,128)(2,1)S(1)} %convolution_convert_fusion.1), channel_id=1, source_target_pairs={{4,0},{8,4},{12,8},{16,12},{20,16},{24,20},{28,24},{0,28},{5,1},{9... | collective-permute-start | bytes 786440 | tf_op jit(solution)/shard_map/ppermute | solution.py:25
  177.6 5.4 %copy-start.2 = (f32[4096,256]{0,1:T(8,128)S(1)}, f32[4096,256]{0,1:T(8,128)}, u32[]{:S(2)}) copy-start(f32[4096,256]{0,1:T(8,128)} %copy-done.1) | copy-start | bytes 12582916
  177.6 5.4 %copy-start.4 = (bf16[4096,256]{0,1:T(8,128)(2,1)S(1)}, bf16[4096,256]{0,1:T(8,128)(2,1)}, u32[]{:S(2)}) copy-start(bf16[4096,256]{0,1:T(8,128)(2,1)} %copy.48) | copy-start | bytes 6291460
  183.0 2.3 copy-start.7
  185.3 2.3 copy-start.25
  187.6 3.0 copy-start.5
  190.6 6.2 %copy-start.3 = (bf16[4096,256]{1,0:T(8,128)(2,1)}, bf16[4096,256]{1,0:T(8,128)(2,1)S(1)}, u32[]{:S(2)}) copy-start(bf16[4096,256]{1,0:T(8,128)(2,1)S(1)} %get-tuple-element.83) | copy-start | bytes 6291460
  190.6 2.3 copy-start.9
  196.8 1.0 copy-start.18
  196.8 1.0 copy-start.19
  196.8 1.1 copy-start.20
  207.9 141.2 %all-reduce.6.cloned.1.call-start = ((), (), s32[]{:S(2)}) async-start(), calls=%async_computation.1 | async-start | bytes 3735552 | tf_op jit(solution)/shard_map/psum | solution.py:217
  284.5 8.2 %copy-start.16 = (f32[1,512,256]{1,2,0:T(8,128)S(1)}, f32[1,512,256]{1,2,0:T(8,128)}, u32[]{:S(2)}) copy-start(f32[1,512,256]{1,2,0:T(8,128)} %get-tuple-element.65) | copy-start | bytes 1572868
  288.7 9.2 %collective-permute-start.6 = (bf16[512,256]{0,1:T(8,128)(2,1)}, bf16[512,256]{0,1:T(8,128)(2,1)S(1)}, u32[]{:S(2)}, u32[]{:S(2)}) collective-permute-start(bf16[512,256]{0,1:T(8,128)(2,1)} %get-tuple-element.63), channel_id=1, source_target_pairs={{0,4},{4,8},{8,12},{12,16},{16,20},{20,24},{24,28},{28,0},{1,5},{5... | collective-permute-start | bytes 786440 | tf_op jit(solution)/shard_map/ppermute | solution.py:35
  288.7 13.0 %collective-permute-start.7 = (bf16[512,256]{0,1:T(8,128)(2,1)}, bf16[512,256]{0,1:T(8,128)(2,1)}, u32[]{:S(2)}, u32[]{:S(2)}) collective-permute-start(bf16[512,256]{0,1:T(8,128)(2,1)} %get-tuple-element.64), channel_id=1, source_target_pairs={{0,28},{4,0},{8,4},{12,8},{16,12},{20,16},{24,20},{28,24},{1,29},{... | collective-permute-start | bytes 786440 | tf_op jit(solution)/shard_map/ppermute | solution.py:35
  293.7 8.0 %copy-start.12 = (bf16[512,256]{1,0:T(8,128)(2,1)S(1)}, bf16[512,256]{1,0:T(8,128)(2,1)}, u32[]{:S(2)}) copy-start(bf16[512,256]{1,0:T(8,128)(2,1)} %copy-done.11) | copy-start | bytes 786436
  303.1 64.7 %copy-start.17 = (f32[456,256]{1,0:T(8,128)S(1)}, f32[456,256]{1,0:T(8,128)}, u32[]{:S(2)}) copy-start(f32[456,256]{1,0:T(8,128)} %param.20) | copy-start | bytes 1400836
  303.1 64.7 %copy-start.22 = (f32[456,256]{1,0:T(8,128)S(1)}, f32[456,256]{1,0:T(8,128)}, u32[]{:S(2)}) copy-start(f32[456,256]{1,0:T(8,128)} %param.23) | copy-start | bytes 1400836
Sparse Core Ops, SparseCore 0:
  208.1 76.3 all-reduce.3
  287.8 61.2 all-reduce.5
